TPU v7x, 32 devices: a whole 2x2x4 slice. The times are simulated.
32 devices in a mesh: row: 8 (over z, y), col: 4 (over x, core).
Axes of the slice: x: 2, y: 2, z: 4, core: 2. Of those that a mesh axis runs over, the one named last changes fastest.
Arguments:
- tensor_ri: bfloat16 [8, 8, 4, 128, 1152], P('row', None, 'col'), may hold values from -6 to 6
- block_mask: int32 [8, 4, 9], P('row', 'col'), may hold values 0 or 1
- green_virt: bfloat16 [8, 4, 128, 3200], P('row', 'col'), may hold values from -0.1875 to 0.1875
- green_occ: bfloat16 [8, 4, 128, 128], P('row', 'col'), may hold values from -0.5 to 0.5
Outputs:
- response: float32 [8, 8], replicated
All inputs are finite; a program needn't handle non-finite values. No bound on the sum of `block_mask` on one device may be relied on, other than what follows from the above.
Results may differ from a plain program's by a relative error of at most 0.0044.
Values may be sent and summed in bfloat16 or wider, within the bound.
A program may use at most 192 MiB of HBM per device.

v0:
```python
import math
import jax
import jax.numpy as jnp
from jax import lax
from jax.sharding import PartitionSpec as P


def extended(cells, sides, width):
    for axis, dim in sides:
        count = lax.axis_size(axis)
        ends = count - 1
        head = lax.slice_in_dim(cells, 0, width, axis=dim)
        tail = lax.slice_in_dim(cells, cells.shape[dim] - width, cells.shape[dim], axis=dim)
        cells = jnp.concatenate(
            [
                lax.ppermute(tail, axis, [(i, (i + 1) % count) for i in range(ends)]),
                cells,
                lax.ppermute(head, axis, [((i + 1) % count, i) for i in range(ends)]),
            ],
            axis=dim,
        )
    return cells


def window_of(band, src_row, src_col, block_width):
    grid_band = band.reshape(block_width, 5, 5, block_width)
    picked = grid_band[:, 2 - src_row : 5 - src_row, 2 - src_col : 5 - src_col, :]
    return picked.reshape(block_width, 9 * block_width)


def per_device(tensor_ri, block_mask, green_virt, green_occ):
    row_count = lax.axis_size("row")
    col_count = lax.axis_size("col")
    block_width = green_occ.shape[-1]
    pair_width = tensor_ri.shape[-1]
    occ_block = green_occ[0, 0]
    regrouped = lax.all_to_all(tensor_ri, "row", split_axis=1, concat_axis=0, tiled=True)
    occ_applied = jnp.einsum(
        "ji,pabiw->pabjw", occ_block, regrouped, preferred_element_type=jnp.float32
    ).astype(jnp.bfloat16)
    rows_all = regrouped.shape[0]
    regrouped = regrouped.reshape(rows_all, block_width, pair_width)
    occ_applied = occ_applied.reshape(rows_all, block_width, pair_width)
    grid_row = lax.axis_index("row")
    grid_col = lax.axis_index("col")
    slots = jnp.arange(9, dtype=jnp.int32)
    near_row = grid_row + slots // 3 - 1
    near_col = grid_col + slots % 3 - 1
    usable = (
        (block_mask[0, 0] == 1)
        & (near_row >= 0)
        & (near_row < row_count)
        & (near_col >= 0)
        & (near_col < col_count)
    )
    kept_slots = jnp.repeat(usable.astype(jnp.bfloat16), block_width)
    regrouped = regrouped * kept_slots
    occ_applied = occ_applied * kept_slots
    windows = []
    rim_blocks = extended(green_virt, (("row", 0), ("col", 1)), 1)
    for source in range(9):
        src_row, src_col = (source // 3, source % 3)
        windows.append(window_of(rim_blocks[src_row, src_col], src_row, src_col, block_width))
    flat_rows = regrouped.reshape(rows_all * block_width, pair_width)
    half_sum = jnp.zeros((rows_all * block_width, pair_width), jnp.float32)
    for source in range(9):
        tile = flat_rows[:, source * block_width : (source + 1) * block_width]
        half_sum = half_sum + jnp.dot(tile, windows[source], preferred_element_type=jnp.float32)
    half_done = half_sum.astype(jnp.bfloat16).reshape(rows_all, block_width * pair_width)
    occ_flat = occ_applied.reshape(rows_all, block_width * pair_width)
    partial_value = lax.dot_general(
        half_done, occ_flat, (((1,), (1,)), ((), ())), preferred_element_type=jnp.float32
    )
    total_basis = block_width * row_count * col_count
    response = lax.psum(partial_value, ("row", "col"))
    return response * (1.0 / math.sqrt(total_basis * 9 * block_width))


def solution(mesh):
    return jax.shard_map(
        per_device,
        mesh=mesh,
        in_specs=(
            P("row", None, "col", None, None),
            P("row", "col", None),
            P("row", "col", None, None),
            P("row", "col", None, None),
        ),
        out_specs=P(),
        check_vma=False,
    )
```

profile of v0, /device:TPU:10, one launch (start us, length us, event | category | flops | bytes accessed | tf_op | source)
XLA Modules:
  0.0 181.1 jit_solution(1390845295951888833)
XLA Ops:
  0.0 1.7 copy.15
  1.7 3.4 %collective-permute-start.1 = (bf16[1,1,128,3200]{2,3,1,0:T(8,128)(2,1)S(1)}, bf16[1,1,128,3200]{2,3,1,0:T(8,128)(2,1)S(1)}, u32[]{:S(2)}, u32[]{:S(2)}) collective-permute-start(bf16[1,1,128,3200]{2,3,1,0:T(8,128)(2,1)S(1)} %copy.15), channel_id=1, source_target_pairs={{4,0},{8,4},{12,8},{16,12},{20,16},{24,20},{28,24},{5,1},{9,5},{13... | collective-permute-start | bytes 2457608 | tf_op jit(solution)/shard_map/ppermute | solution.py:18
  5.2 2.5 %collective-permute-start = (bf16[1,1,128,3200]{2,3,1,0:T(8,128)(2,1)S(1)}, bf16[1,1,128,3200]{2,3,1,0:T(8,128)(2,1)S(1)}, u32[]{:S(2)}, u32[]{:S(2)}) collective-permute-start(bf16[1,1,128,3200]{2,3,1,0:T(8,128)(2,1)S(1)} %copy.15), channel_id=1, source_target_pairs={{0,4},{4,8},{8,12},{12,16},{16,20},{20,24},{24,28},{1,5},{5,9},{9,... | collective-permute-start | bytes 2457608 | tf_op jit(solution)/shard_map/ppermute | solution.py:16
  7.7 33.6 %collective-permute-done.1 = bf16[1,1,128,3200]{2,3,1,0:T(8,128)(2,1)S(1)} collective-permute-done((bf16[1,1,128,3200]{2,3,1,0:T(8,128)(2,1)S(1)}, bf16[1,1,128,3200]{2,3,1,0:T(8,128)(2,1)S(1)}, u32[]{:S(2)}, u32[]{:S(2)}) %collective-permute-start.1) | collective-permute-done | bytes 819232 | tf_op jit(solution)/shard_map/ppermute | solution.py:18
  42.2 1.7 pad_maximum_fusion
  43.9 1.9 %collective-permute-start.3 = (bf16[3,1,128,3200]{2,3,1,0:T(8,128)(2,1)}, bf16[3,1,128,3200]{2,3,1,0:T(8,128)(2,1)}, u32[]{:S(2)}, u32[]{:S(2)}) collective-permute-start(bf16[3,1,128,3200]{2,3,1,0:T(8,128)(2,1)} %pad_maximum_fusion), channel_id=1, source_target_pairs={{1,0},{2,1},{3,2},{5,4},{6,5},{7,6},{9,8},{10,9},{11,10},{13,12},{... | collective-permute-start | bytes 7372808 | tf_op jit(solution)/shard_map/ppermute | solution.py:18
  45.9 2.6 %copy.13 = bf16[1,8,1,128,1152]{3,4,2,0,1:T(8,128)(2,1)} copy(bf16[1,8,1,128,1152]{4,3,2,1,0:T(8,128)(2,1)S(1)} %copy-done.3) | data formatting | bytes 4718592 | tf_op args[0]
  48.4 5.5 %all-to-all-start = ((bf16[1,8,1,128,1152]{3,4,2,0,1:T(8,128)(2,1)}), bf16[1,8,1,128,1152]{3,4,2,0,1:T(8,128)(2,1)S(1)}, u32[]{:S(2)}, u32[]{:S(2)}) async-start(bf16[1,8,1,128,1152]{3,4,2,0,1:T(8,128)(2,1)} %copy.13), calls=%async_computation | async-start | bytes 4718592 | tf_op jit(solution)/shard_map/all_to_all | solution.py:37
  54.0 3.2 %collective-permute-start.2 = (bf16[3,1,128,3200]{2,3,1,0:T(8,128)(2,1)}, bf16[3,1,128,3200]{2,3,1,0:T(8,128)(2,1)}, u32[]{:S(2)}, u32[]{:S(2)}) collective-permute-start(bf16[3,1,128,3200]{2,3,1,0:T(8,128)(2,1)} %pad_maximum_fusion), channel_id=1, source_target_pairs={{0,1},{1,2},{2,3},{4,5},{5,6},{6,7},{8,9},{9,10},{10,11},{12,13},{... | collective-permute-start | bytes 7372808 | tf_op jit(solution)/shard_map/ppermute | solution.py:16
  58.3 1.7 slice.100
  60.0 13.6 %collective-permute-done.3 = bf16[3,1,128,3200]{2,3,1,0:T(8,128)(2,1)} collective-permute-done((bf16[3,1,128,3200]{2,3,1,0:T(8,128)(2,1)}, bf16[3,1,128,3200]{2,3,1,0:T(8,128)(2,1)}, u32[]{:S(2)}, u32[]{:S(2)}) %collective-permute-start.3) | collective-permute-done | bytes 2457632 | tf_op jit(solution)/shard_map/ppermute | solution.py:18
  73.6 1.8 fusion.27
  76.9 8.6 %collective-permute-done.2 = bf16[3,1,128,3200]{2,3,1,0:T(8,128)(2,1)} collective-permute-done((bf16[3,1,128,3200]{2,3,1,0:T(8,128)(2,1)}, bf16[3,1,128,3200]{2,3,1,0:T(8,128)(2,1)}, u32[]{:S(2)}, u32[]{:S(2)}) %collective-permute-start.2) | collective-permute-done | bytes 2457632 | tf_op jit(solution)/shard_map/ppermute | solution.py:16
  85.5 1.8 fusion.26
  89.5 17.2 %all-to-all-done = bf16[1,8,1,128,1152]{3,4,2,0,1:T(8,128)(2,1)S(1)} async-done(((bf16[1,8,1,128,1152]{3,4,2,0,1:T(8,128)(2,1)}), bf16[1,8,1,128,1152]{3,4,2,0,1:T(8,128)(2,1)S(1)}, u32[]{:S(2)}, u32[]{:S(2)}) %all-to-all-start) | async-done | bytes 2359328 | tf_op jit(solution)/shard_map/all_to_all | solution.py:37
  106.7 2.6 %copy.14 = bf16[1,8,1,128,1152]{4,3,1,2,0:T(8,128)(2,1)} copy(bf16[1,8,1,128,1152]{3,4,2,0,1:T(8,128)(2,1)S(1)} %all-to-all-done) | data formatting | bytes 4718592 | tf_op jit(solution)/shard_map/all_to_all | solution.py:37
  109.3 3.3 %bitcast_multiply_fusion = bf16[1024,1152]{1,0:T(8,128)(2,1)} fusion(bf16[1,8,1,128,1152]{4,3,1,2,0:T(8,128)(2,1)} %copy.14, bf16[1152]{0:T(1024)(128)(2,1)S(1)} %broadcast_bitcast_fusion), kind=kLoop, calls=%fused_computation.15 | loop fusion | flops 1179648 | bytes 4720896 | tf_op jit(solution)/shard_map/mul | solution.py:57
  112.6 2.2 %fusion.4 = bf16[8,1,1,128,1152]{3,4,0,2,1:T(8,128)(2,1)} fusion(bf16[1,8,1,128,1152]{3,4,2,0,1:T(8,128)(2,1)S(1)} %all-to-all-done, bf16[1152]{0:T(1024)(128)(2,1)S(1)} %broadcast_bitcast_fusion, bf16[1,1,128,128]{3,2,1,0:T(8,128)(2,1)S(1)} %copy-done), kind=kOutput, calls=%fused_computation.12 | convolution fusion | flops 304349184 | bytes 4753664 | tf_op jit(solution)/shard_map/ji,pabiw->pabjw/dot_general | solution.py:38
  114.8 4.3 %copy.19 = bf16[8,1,1,128,1152]{4,3,0,2,1:T(8,128)(2,1)} copy(bf16[8,1,1,128,1152]{3,4,0,2,1:T(8,128)(2,1)} %fusion.4) | data formatting | bytes 4718592 | tf_op jit(solution)/shard_map/mul | solution.py:58
  119.1 3.1 %copy.20 = bf16[1,8,128,1152]{3,1,2,0:T(8,128)(2,1)S(1)} copy(bf16[1,8,128,1152]{3,2,1,0:T(8,128)(2,1)} %bitcast.64) | data formatting | bytes 4718592
  129.5 2.2 %fusion.1 = bf16[1024,1152]{1,0:T(8,128)(2,1)} fusion(f32[1024,1152]{1,0:T(8,128)S(1)} %fusion.6, f32[1024,1152]{1,0:T(8,128)S(1)} %convolution_add_fusion.1, bf16[128,1152]{0,1:T(8,128)(2,1)S(1)} %bitcast.74, bf16[1024,1152]{1,0:T(8,128)(2,1)S(1)} %copy-done.2), kind=kOutput, calls=%fused_computation.8 | convolution fusion | flops 305528832 | bytes 12353536 | tf_op jit(solution)/shard_map/dot_general | solution.py:68
  131.7 4.1 %reshape.69 = bf16[8,147456]{1,0:T(8,128)(2,1)} reshape(bf16[1024,1152]{1,0:T(8,128)(2,1)} %fusion.1) | data formatting | bytes 4718592 | tf_op jit(solution)/shard_map/reshape | solution.py:69
  135.9 3.3 %fusion.28 = f32[8,8]{1,0:T(8,128)S(1)} fusion(bf16[8,147456]{1,0:T(8,128)(2,1)} %reshape.69, bf16[8,147456]{1,0:T(8,128)(2,1)S(1)} %bitcast.63), kind=kOutput, calls=%fused_computation.46 | convolution fusion | flops 18874368 | bytes 4718848 | tf_op jit(solution)/shard_map/dot_general | solution.py:71
  139.1 41.3 %psum.7 = f32[8,8]{1,0:T(8,128)S(1)} all-reduce(f32[8,8]{1,0:T(8,128)S(1)} %fusion.28), channel_id=1, replica_groups=mesh['row'=8,'col'=4] {'row','col'}, use_global_device_ids=true, to_apply=%region_0.1 | all-reduce | flops 64 | bytes 512 | tf_op jit(solution)/shard_map/psum | solution.py:75
  (46 shorter events, 13.5 us)
Async XLA Ops:
  0.0 112.6 %copy-start = (bf16[1,1,128,128]{3,2,1,0:T(8,128)(2,1)S(1)}, bf16[1,1,128,128]{3,2,1,0:T(8,128)(2,1)}, u32[]{:S(2)}) copy-start(bf16[1,1,128,128]{3,2,1,0:T(8,128)(2,1)} %param.7) | copy-start | bytes 98308
  1.7 44.1 %copy-start.3 = (bf16[1,8,1,128,1152]{4,3,2,1,0:T(8,128)(2,1)S(1)}, bf16[1,8,1,128,1152]{4,3,2,1,0:T(8,128)(2,1)}, u32[]{:S(2)}) copy-start(bf16[1,8,1,128,1152]{4,3,2,1,0:T(8,128)(2,1)} %param.4) | copy-start | bytes 7077892
  1.7 39.6 %collective-permute-start.1 = (bf16[1,1,128,3200]{2,3,1,0:T(8,128)(2,1)S(1)}, bf16[1,1,128,3200]{2,3,1,0:T(8,128)(2,1)S(1)}, u32[]{:S(2)}, u32[]{:S(2)}) collective-permute-start(bf16[1,1,128,3200]{2,3,1,0:T(8,128)(2,1)S(1)} %copy.15), channel_id=1, source_target_pairs={{4,0},{8,4},{12,8},{16,12},{20,16},{24,20},{28,24},{5,1},{9,5},{13... | collective-permute-start | bytes 2457608 | tf_op jit(solution)/shard_map/ppermute | solution.py:18
  5.2 36.1 %collective-permute-start = (bf16[1,1,128,3200]{2,3,1,0:T(8,128)(2,1)S(1)}, bf16[1,1,128,3200]{2,3,1,0:T(8,128)(2,1)S(1)}, u32[]{:S(2)}, u32[]{:S(2)}) collective-permute-start(bf16[1,1,128,3200]{2,3,1,0:T(8,128)(2,1)S(1)} %copy.15), channel_id=1, source_target_pairs={{0,4},{4,8},{8,12},{12,16},{16,20},{20,24},{24,28},{1,5},{5,9},{9,... | collective-permute-start | bytes 2457608 | tf_op jit(solution)/shard_map/ppermute | solution.py:16
  41.3 0.9 copy-start.4
  42.2 1.7 copy-start.5
  43.9 29.6 %collective-permute-start.3 = (bf16[3,1,128,3200]{2,3,1,0:T(8,128)(2,1)}, bf16[3,1,128,3200]{2,3,1,0:T(8,128)(2,1)}, u32[]{:S(2)}, u32[]{:S(2)}) collective-permute-start(bf16[3,1,128,3200]{2,3,1,0:T(8,128)(2,1)} %pad_maximum_fusion), channel_id=1, source_target_pairs={{1,0},{2,1},{3,2},{5,4},{6,5},{7,6},{9,8},{10,9},{11,10},{13,12},{... | collective-permute-start | bytes 7372808 | tf_op jit(solution)/shard_map/ppermute | solution.py:18
  48.4 8.8 %copy-start.12 = (s32[1,1,9]{2,1,0:T(1,128)S(1)}, s32[1,1,9]{2,1,0:T(1,128)}, u32[]{:S(2)}) copy-start(s32[1,1,9]{2,1,0:T(1,128)} %param.5) | copy-start | bytes 112
  48.4 58.3 %all-to-all-start = ((bf16[1,8,1,128,1152]{3,4,2,0,1:T(8,128)(2,1)}), bf16[1,8,1,128,1152]{3,4,2,0,1:T(8,128)(2,1)S(1)}, u32[]{:S(2)}, u32[]{:S(2)}) async-start(bf16[1,8,1,128,1152]{3,4,2,0,1:T(8,128)(2,1)} %copy.13), calls=%async_computation | async-start | bytes 4718592 | tf_op jit(solution)/shard_map/all_to_all | solution.py:37
  54.0 31.5 %collective-permute-start.2 = (bf16[3,1,128,3200]{2,3,1,0:T(8,128)(2,1)}, bf16[3,1,128,3200]{2,3,1,0:T(8,128)(2,1)}, u32[]{:S(2)}, u32[]{:S(2)}) collective-permute-start(bf16[3,1,128,3200]{2,3,1,0:T(8,128)(2,1)} %pad_maximum_fusion), channel_id=1, source_target_pairs={{0,1},{1,2},{2,3},{4,5},{5,6},{6,7},{8,9},{9,10},{10,11},{12,13},{... | collective-permute-start | bytes 7372808 | tf_op jit(solution)/shard_map/ppermute | solution.py:16
  119.1 3.1 %copy-start.2 = (bf16[1024,1152]{1,0:T(8,128)(2,1)S(1)}, bf16[1024,1152]{1,0:T(8,128)(2,1)}, u32[]{:S(2)}) copy-start(bf16[1024,1152]{1,0:T(8,128)(2,1)} %bitcast_multiply_fusion) | copy-start | bytes 7077892
  119.1 3.1 %copy-start.9 = (bf16[128,3,3,128]{0,3,2,1:T(8,128)(2,1)S(1)}, bf16[128,3,3,128]{0,3,2,1:T(8,128)(2,1)}, u32[]{:S(2)}) copy-start(bf16[128,3,3,128]{0,3,2,1:T(8,128)(2,1)} %slice.119) | copy-start | bytes 884740
  122.3 1.0 copy-start.6
  123.3 1.0 copy-start.11
  124.2 1.0 copy-start.8
  125.2 1.0 copy-start.10
  127.7 1.0 copy-start.7
  131.7 49.4 %copy-start.1 = (bf16[1,1,128,128]{3,2,1,0:T(8,128)(2,1)S(1)}, bf16[1,1,128,128]{3,2,1,0:T(8,128)(2,1)}, u32[]{:S(2)}) copy-start(bf16[1,1,128,128]{3,2,1,0:T(8,128)(2,1)} %param.7) | copy-start | bytes 98308
where the time goes:
time: 182 us; the launch traced here: 181 us
  waiting for transfers between devices  72.9 us (40%)
  blocking collectives  41.3 us (23%)
  local copies, waits for them, and re-layouts  30.4 us (17%)
  starting transfers between devices  16.6 us (9%)
  matrix products  14 us (8%)
  other arithmetic  5.65 us (3%)
    ppermute x2, waiting for transfers between devices, extended(): lax.ppermute(head, axis, [((i + 1) % count, i) for i in range(ends)])  47.1 us
    psum x1, blocking collectives, per_device(): response = lax.psum(partial_value, ('row', 'col'))  41.3 us
    all_to_all x1, waiting for transfers between devices, per_device(): lax.all_to_all(tensor_ri, 'row', split_axis=1, concat_axis=0, tiled=True)  17.2 us
    unnamed x29, local copies, waits for them, and re-layouts  9.19 us
    ppermute x2, waiting for transfers between devices, extended(): lax.ppermute(tail, axis, [(i, (i + 1) % count) for i in range(ends)])  8.6 us
    dot_general x9, matrix products, per_device(): jnp.dot(tile, windows[source], preferred_element_type=jnp.float32)  8.5 us
    slice x9, local copies, waits for them, and re-layouts, window_of(): picked = grid_band[:, 2 - src_row:5 - src_row, 2 - src_col:5 - src_col, :]  6.45 us
    ppermute x2, starting transfers between devices, extended(): lax.ppermute(tail, axis, [(i, (i + 1) % count) for i in range(ends)])  5.74 us
  transfers between devices with their start and end apart: 5, of which 4 were waited for; matrix products, arithmetic and copies ran while one was open for 7% of the time, Pallas kernels for 0%

commit v1 on v0

--- a/solution.py
+++ b/solution.py
@@ -72,7 +72,7 @@
         half_done, occ_flat, (((1,), (1,)), ((), ())), preferred_element_type=jnp.float32
     )
     total_basis = block_width * row_count * col_count
-    response = lax.psum(partial_value, ("row", "col"))
+    response = jnp.sum(lax.all_gather(partial_value, ("row", "col")), axis=0)
     return response * (1.0 / math.sqrt(total_basis * 9 * block_width))
 
 

time: 182 us -> 184 us (1.011)
  the two profiles are of different devices: /device:TPU:10 before, /device:TPU:0 now
where the time goes in v1:
time: 184 us; the launch traced here: 183 us
  waiting for transfers between devices  75 us (41%)
  blocking collectives  40.4 us (22%)
  local copies, waits for them, and re-layouts  29.5 us (16%)
  starting transfers between devices  18.5 us (10%)
  matrix products  14 us (8%)
  other arithmetic  5.69 us (3%)
    all_to_all x1, waiting for transfers between devices, per_device(): lax.all_to_all(tensor_ri, 'row', split_axis=1, concat_axis=0, tiled=True)  41 us
    all_gather x1, blocking collectives, per_device(): response = jnp.sum(lax.all_gather(partial_value, ('row', 'col')), axis=0)  40.4 us
    ppermute x2, waiting for transfers between devices, extended(): lax.ppermute(tail, axis, [(i, (i + 1) % count) for i in range(ends)])  17.7 us
    ppermute x2, waiting for transfers between devices, extended(): lax.ppermute(head, axis, [((i + 1) % count, i) for i in range(ends)])  16.3 us
    ppermute x2, starting transfers between devices, extended(): lax.ppermute(tail, axis, [(i, (i + 1) % count) for i in range(ends)])  9.79 us
    dot_general x9, matrix products, per_device(): jnp.dot(tile, windows[source], preferred_element_type=jnp.float32)  8.48 us
    unnamed x29, local copies, waits for them, and re-layouts  8.29 us
    slice x9, local copies, waits for them, and re-layouts, window_of(): picked = grid_band[:, 2 - src_row:5 - src_row, 2 - src_col:5 - src_col, :]  6.45 us
  transfers between devices with their start and end apart: 5, of which 3 were waited for; matrix products, arithmetic and copies ran while one was open for 7% of the time, Pallas kernels for 0%

profile of v1, /device:TPU:0, one launch (start us, length us, event | category | flops | bytes accessed | tf_op | source)
XLA Modules:
  0.0 183.2 jit_solution(15184007008995038226)
XLA Ops:
  0.0 1.7 copy.15
  1.7 1.4 collective-permute-start.1
  3.2 5.6 %collective-permute-start = (bf16[1,1,128,3200]{2,3,1,0:T(8,128)(2,1)S(1)}, bf16[1,1,128,3200]{2,3,1,0:T(8,128)(2,1)S(1)}, u32[]{:S(2)}, u32[]{:S(2)}) collective-permute-start(bf16[1,1,128,3200]{2,3,1,0:T(8,128)(2,1)S(1)} %copy.15), channel_id=1, source_target_pairs={{0,4},{4,8},{8,12},{12,16},{16,20},{20,24},{24,28},{1,5},{5,9},{9,... | collective-permute-start | bytes 2457608 | tf_op jit(solution)/shard_map/ppermute | solution.py:16
  8.7 16.3 %collective-permute-done.1 = bf16[1,1,128,3200]{2,3,1,0:T(8,128)(2,1)S(1)} collective-permute-done((bf16[1,1,128,3200]{2,3,1,0:T(8,128)(2,1)S(1)}, bf16[1,1,128,3200]{2,3,1,0:T(8,128)(2,1)S(1)}, u32[]{:S(2)}, u32[]{:S(2)}) %collective-permute-start.1) | collective-permute-done | bytes 819232 | tf_op jit(solution)/shard_map/ppermute | solution.py:18
  25.0 17.7 %collective-permute-done = bf16[1,1,128,3200]{2,3,1,0:T(8,128)(2,1)S(1)} collective-permute-done((bf16[1,1,128,3200]{2,3,1,0:T(8,128)(2,1)S(1)}, bf16[1,1,128,3200]{2,3,1,0:T(8,128)(2,1)S(1)}, u32[]{:S(2)}, u32[]{:S(2)}) %collective-permute-start) | collective-permute-done | bytes 819232 | tf_op jit(solution)/shard_map/ppermute | solution.py:16
  42.7 1.7 pad_maximum_fusion
  44.4 1.3 collective-permute-start.3
  45.7 2.6 %copy.13 = bf16[1,8,1,128,1152]{3,4,2,0,1:T(8,128)(2,1)} copy(bf16[1,8,1,128,1152]{4,3,2,1,0:T(8,128)(2,1)S(1)} %copy-done.3) | data formatting | bytes 4718592 | tf_op args[0]
  48.3 6.0 %all-to-all-start = ((bf16[1,8,1,128,1152]{3,4,2,0,1:T(8,128)(2,1)}), bf16[1,8,1,128,1152]{3,4,2,0,1:T(8,128)(2,1)S(1)}, u32[]{:S(2)}, u32[]{:S(2)}) async-start(bf16[1,8,1,128,1152]{3,4,2,0,1:T(8,128)(2,1)} %copy.13), calls=%async_computation | async-start | bytes 4718592 | tf_op jit(solution)/shard_map/all_to_all | solution.py:37
  54.3 4.2 %collective-permute-start.2 = (bf16[3,1,128,3200]{2,3,1,0:T(8,128)(2,1)}, bf16[3,1,128,3200]{2,3,1,0:T(8,128)(2,1)}, u32[]{:S(2)}, u32[]{:S(2)}) collective-permute-start(bf16[3,1,128,3200]{2,3,1,0:T(8,128)(2,1)} %pad_maximum_fusion), channel_id=1, source_target_pairs={{0,1},{1,2},{2,3},{4,5},{5,6},{6,7},{8,9},{9,10},{10,11},{12,13},{... | collective-permute-start | bytes 7372808 | tf_op jit(solution)/shard_map/ppermute | solution.py:16
  58.6 1.0 slice.116
  59.6 1.7 slice.100
  61.3 1.8 fusion.27
  64.6 1.8 fusion.26
  68.7 41.0 %all-to-all-done = bf16[1,8,1,128,1152]{3,4,2,0,1:T(8,128)(2,1)S(1)} async-done(((bf16[1,8,1,128,1152]{3,4,2,0,1:T(8,128)(2,1)}), bf16[1,8,1,128,1152]{3,4,2,0,1:T(8,128)(2,1)S(1)}, u32[]{:S(2)}, u32[]{:S(2)}) %all-to-all-start) | async-done | bytes 2359328 | tf_op jit(solution)/shard_map/all_to_all | solution.py:37
  109.7 2.6 %copy.14 = bf16[1,8,1,128,1152]{4,3,1,2,0:T(8,128)(2,1)} copy(bf16[1,8,1,128,1152]{3,4,2,0,1:T(8,128)(2,1)S(1)} %all-to-all-done) | data formatting | bytes 4718592 | tf_op jit(solution)/shard_map/all_to_all | solution.py:37
  112.3 3.3 %bitcast_multiply_fusion = bf16[1024,1152]{1,0:T(8,128)(2,1)} fusion(bf16[1,8,1,128,1152]{4,3,1,2,0:T(8,128)(2,1)} %copy.14, bf16[1152]{0:T(1024)(128)(2,1)S(1)} %broadcast_bitcast_fusion), kind=kLoop, calls=%fused_computation.15 | loop fusion | flops 1179648 | bytes 4720896 | tf_op jit(solution)/shard_map/mul | solution.py:57
  115.6 2.2 %fusion.4 = bf16[8,1,1,128,1152]{3,4,0,2,1:T(8,128)(2,1)} fusion(bf16[1,8,1,128,1152]{3,4,2,0,1:T(8,128)(2,1)S(1)} %all-to-all-done, bf16[1152]{0:T(1024)(128)(2,1)S(1)} %broadcast_bitcast_fusion, bf16[1,1,128,128]{3,2,1,0:T(8,128)(2,1)S(1)} %copy-done), kind=kOutput, calls=%fused_computation.12 | convolution fusion | flops 304349184 | bytes 4753664 | tf_op jit(solution)/shard_map/ji,pabiw->pabjw/dot_general | solution.py:38
  117.8 4.3 %copy.19 = bf16[8,1,1,128,1152]{4,3,0,2,1:T(8,128)(2,1)} copy(bf16[8,1,1,128,1152]{3,4,0,2,1:T(8,128)(2,1)} %fusion.4) | data formatting | bytes 4718592 | tf_op jit(solution)/shard_map/mul | solution.py:58
  122.1 3.1 %copy.20 = bf16[1,8,128,1152]{3,1,2,0:T(8,128)(2,1)S(1)} copy(bf16[1,8,128,1152]{3,2,1,0:T(8,128)(2,1)} %bitcast.66) | data formatting | bytes 4718592
  132.5 2.2 %fusion.1 = bf16[1024,1152]{1,0:T(8,128)(2,1)} fusion(f32[1024,1152]{1,0:T(8,128)S(1)} %fusion.6, f32[1024,1152]{1,0:T(8,128)S(1)} %convolution_add_fusion.1, bf16[128,1152]{0,1:T(8,128)(2,1)S(1)} %bitcast.76, bf16[1024,1152]{1,0:T(8,128)(2,1)S(1)} %copy-done.2), kind=kOutput, calls=%fused_computation.8 | convolution fusion | flops 305528832 | bytes 12353536 | tf_op jit(solution)/shard_map/dot_general | solution.py:68
  134.7 4.1 %reshape.69 = bf16[8,147456]{1,0:T(8,128)(2,1)} reshape(bf16[1024,1152]{1,0:T(8,128)(2,1)} %fusion.1) | data formatting | bytes 4718592 | tf_op jit(solution)/shard_map/reshape | solution.py:69
  138.8 3.3 %fusion.28 = f32[8,8]{1,0:T(8,128)S(1)} fusion(bf16[8,147456]{1,0:T(8,128)(2,1)} %reshape.69, bf16[8,147456]{1,0:T(8,128)(2,1)S(1)} %bitcast.65), kind=kOutput, calls=%fused_computation.47 | convolution fusion | flops 18874368 | bytes 4718848 | tf_op jit(solution)/shard_map/dot_general | solution.py:71
  142.1 40.4 %all-gather = f32[256,8]{1,0:T(8,128)S(1)} all-gather(f32[8,8]{1,0:T(8,128)S(1)} %fusion.28), channel_id=2, replica_groups=mesh['row'=8,'col'=4] {'row','col'}, dimensions={0}, use_global_device_ids=true | all-gather | bytes 8448 | tf_op jit(solution)/shard_map/all_gather | solution.py:75
  (47 shorter events, 11.7 us)
Async XLA Ops:
  0.0 115.6 %copy-start = (bf16[1,1,128,128]{3,2,1,0:T(8,128)(2,1)S(1)}, bf16[1,1,128,128]{3,2,1,0:T(8,128)(2,1)}, u32[]{:S(2)}) copy-start(bf16[1,1,128,128]{3,2,1,0:T(8,128)(2,1)} %param.7) | copy-start | bytes 98308
  1.7 44.0 %copy-start.3 = (bf16[1,8,1,128,1152]{4,3,2,1,0:T(8,128)(2,1)S(1)}, bf16[1,8,1,128,1152]{4,3,2,1,0:T(8,128)(2,1)}, u32[]{:S(2)}) copy-start(bf16[1,8,1,128,1152]{4,3,2,1,0:T(8,128)(2,1)} %param.4) | copy-start | bytes 7077892
  1.7 23.2 %collective-permute-start.1 = (bf16[1,1,128,3200]{2,3,1,0:T(8,128)(2,1)S(1)}, bf16[1,1,128,3200]{2,3,1,0:T(8,128)(2,1)S(1)}, u32[]{:S(2)}, u32[]{:S(2)}) collective-permute-start(bf16[1,1,128,3200]{2,3,1,0:T(8,128)(2,1)S(1)} %copy.15), channel_id=1, source_target_pairs={{4,0},{8,4},{12,8},{16,12},{20,16},{24,20},{28,24},{5,1},{9,5},{13... | collective-permute-start | bytes 2457608 | tf_op jit(solution)/shard_map/ppermute | solution.py:18
  3.2 39.5 %collective-permute-start = (bf16[1,1,128,3200]{2,3,1,0:T(8,128)(2,1)S(1)}, bf16[1,1,128,3200]{2,3,1,0:T(8,128)(2,1)S(1)}, u32[]{:S(2)}, u32[]{:S(2)}) collective-permute-start(bf16[1,1,128,3200]{2,3,1,0:T(8,128)(2,1)S(1)} %copy.15), channel_id=1, source_target_pairs={{0,4},{4,8},{8,12},{12,16},{16,20},{20,24},{24,28},{1,5},{5,9},{9,... | collective-permute-start | bytes 2457608 | tf_op jit(solution)/shard_map/ppermute | solution.py:16
  25.0 17.7 %copy-start.4 = (bf16[1,1,128,3200]{2,3,1,0:T(8,128)(2,1)}, bf16[1,1,128,3200]{2,3,1,0:T(8,128)(2,1)S(1)}, u32[]{:S(2)}) copy-start(bf16[1,1,128,3200]{2,3,1,0:T(8,128)(2,1)S(1)} %collective-permute-done.1) | copy-start | bytes 2457604
  42.7 1.7 copy-start.5
  44.4 16.9 %collective-permute-start.3 = (bf16[3,1,128,3200]{2,3,1,0:T(8,128)(2,1)}, bf16[3,1,128,3200]{2,3,1,0:T(8,128)(2,1)}, u32[]{:S(2)}, u32[]{:S(2)}) collective-permute-start(bf16[3,1,128,3200]{2,3,1,0:T(8,128)(2,1)} %pad_maximum_fusion), channel_id=1, source_target_pairs={{1,0},{2,1},{3,2},{5,4},{6,5},{7,6},{9,8},{10,9},{11,10},{13,12},{... | collective-permute-start | bytes 7372808 | tf_op jit(solution)/shard_map/ppermute | solution.py:18
  48.3 10.2 %copy-start.12 = (s32[1,1,9]{2,1,0:T(1,128)S(1)}, s32[1,1,9]{2,1,0:T(1,128)}, u32[]{:S(2)}) copy-start(s32[1,1,9]{2,1,0:T(1,128)} %param.5) | copy-start | bytes 112
  48.3 61.4 %all-to-all-start = ((bf16[1,8,1,128,1152]{3,4,2,0,1:T(8,128)(2,1)}), bf16[1,8,1,128,1152]{3,4,2,0,1:T(8,128)(2,1)S(1)}, u32[]{:S(2)}, u32[]{:S(2)}) async-start(bf16[1,8,1,128,1152]{3,4,2,0,1:T(8,128)(2,1)} %copy.13), calls=%async_computation | async-start | bytes 4718592 | tf_op jit(solution)/shard_map/all_to_all | solution.py:37
  54.3 10.4 %collective-permute-start.2 = (bf16[3,1,128,3200]{2,3,1,0:T(8,128)(2,1)}, bf16[3,1,128,3200]{2,3,1,0:T(8,128)(2,1)}, u32[]{:S(2)}, u32[]{:S(2)}) collective-permute-start(bf16[3,1,128,3200]{2,3,1,0:T(8,128)(2,1)} %pad_maximum_fusion), channel_id=1, source_target_pairs={{0,1},{1,2},{2,3},{4,5},{5,6},{6,7},{8,9},{9,10},{10,11},{12,13},{... | collective-permute-start | bytes 7372808 | tf_op jit(solution)/shard_map/ppermute | solution.py:16
  122.1 3.1 %copy-start.2 = (bf16[1024,1152]{1,0:T(8,128)(2,1)S(1)}, bf16[1024,1152]{1,0:T(8,128)(2,1)}, u32[]{:S(2)}) copy-start(bf16[1024,1152]{1,0:T(8,128)(2,1)} %bitcast_multiply_fusion) | copy-start | bytes 7077892
  122.1 3.1 %copy-start.9 = (bf16[128,3,3,128]{0,3,2,1:T(8,128)(2,1)S(1)}, bf16[128,3,3,128]{0,3,2,1:T(8,128)(2,1)}, u32[]{:S(2)}) copy-start(bf16[128,3,3,128]{0,3,2,1:T(8,128)(2,1)} %slice.119) | copy-start | bytes 884740
  125.3 1.0 copy-start.6
  126.2 1.0 copy-start.11
  127.2 1.0 copy-start.8
  128.1 1.0 copy-start.10
  130.7 1.0 copy-start.7
  138.8 44.4 %copy-start.1 = (bf16[1,1,128,128]{3,2,1,0:T(8,128)(2,1)S(1)}, bf16[1,1,128,128]{3,2,1,0:T(8,128)(2,1)}, u32[]{:S(2)}) copy-start(bf16[1,1,128,128]{3,2,1,0:T(8,128)(2,1)} %param.7) | copy-start | bytes 98308
